TPU v7x, 32 devices: a whole 2x2x4 slice. The times are simulated.
32 devices in a mesh: rep: 8 (over z, y), col: 4 (over x, core).
Axes of the slice: x: 2, y: 2, z: 4, core: 2. Of those that a mesh axis runs over, the one named last changes fastest.
Arguments:
- momentum: float32 [8, 288, 8192], P('rep', None, 'col'), may hold values from -6 to 6
- grads: bfloat16 [2, 8, 288, 8192], P(None, 'rep', None, 'col'), may hold values from -3 to 3
- weights: float32 [288, 8192], P(None, 'col'), may hold values from -6 to 6
- right_factor: float32 [8192, 256], P('col'), may hold values from -0.0625 to 0.0625
Outputs:
- new_weights: float32 [288, 8192], P(None, 'col')
- new_momentum: float32 [8, 288, 8192], P('rep', None, 'col')
- new_right: float32 [8192, 256], P('col')
All inputs are finite; a program needn't handle non-finite values.
Results may differ from a plain program's by a relative error of at most 0.0003.
Values sent between devices are 32-bit elements; how exact they have to be, the bound alone decides.
No kernel may reach another device: no remote copies, remote signals or barrier semaphores. Data moves between devices by JAX's collectives and lax.ppermute only.
A program may use at most 64 MiB of HBM per device.

v0:
```python
import math
import jax
import jax.numpy as jnp
from jax import lax
from jax.sharding import PartitionSpec as P

ROWS = 288
N = 8192
R = 256
STEPS = 2
precise = lax.Precision.HIGHEST
damping = 0.1
rate_base = 0.2
epsilon = 1e-06


def orthonormal(left_raw):
    gram_matrix = jnp.dot(left_raw.T, left_raw, precision=precise)
    lower_factor = jnp.linalg.cholesky(gram_matrix)
    return jax.scipy.linalg.solve_triangular(lower_factor, left_raw.T, lower=True).T


def transposed(matrix, left_factor):
    return lax.dot_general(matrix, left_factor, (((0,), (0,)), ((), ())), precision=precise)


def column_unit(right_raw):
    squares = jnp.sum(right_raw * right_raw, axis=0)
    totals = lax.psum(squares, "col")
    return right_raw / jnp.sqrt(totals + epsilon)


def finish(combined, left_factor, right_raw, weight_now):
    correction = jnp.dot(left_factor, right_raw.T, precision=precise)
    moment = combined - damping * correction
    right_factor = column_unit(right_raw)
    step_size = rate_base * math.sqrt(ROWS * N / R)
    weight_now = weight_now - step_size * jnp.dot(left_factor, right_factor.T, precision=precise)
    return (moment, right_factor, weight_now, correction)


def shards(momentum, grads, weights, right_factor):
    replicas = lax.axis_size("rep")
    moment = momentum[0]
    weight_now = weights
    first_sum = moment + grads[0, 0].astype(jnp.float32)
    summed = (
        lax.psum_scatter(first_sum, "rep", scatter_dimension=1, tiled=True),
        lax.psum_scatter(grads[1, 0].astype(jnp.float32), "rep", scatter_dimension=1, tiled=True),
    )
    averaged, grad_mean = (
        lax.all_gather(summed[0] / replicas, "rep", axis=1, tiled=True),
        lax.all_gather(summed[1] / replicas, "rep", axis=1, tiled=True),
    )
    combined = first_sum
    for section_index in range(STEPS):
        if section_index > 0:
            combined = moment + grads[section_index, 0].astype(jnp.float32)
        left_raw = lax.psum(jnp.dot(averaged, right_factor, precision=precise), "col")
        left_factor = orthonormal(left_raw)
        right_raw = transposed(averaged, left_factor)
        moment, right_factor, weight_now, correction = finish(
            combined, left_factor, right_raw, weight_now
        )
        averaged = averaged - damping * correction + grad_mean
    return (weight_now, moment[None], right_factor)


def solution(mesh):
    return jax.shard_map(
        shards,
        mesh=mesh,
        in_specs=(
            P("rep", None, "col"),
            P(None, "rep", None, "col"),
            P(None, "col"),
            P("col", None),
        ),
        out_specs=(P(None, "col"), P("rep", None, "col"), P("col", None)),
        check_vma=False,
    )
```

profile of v0, /device:TPU:0, one launch (start us, length us, event | category | flops | bytes accessed | tf_op | source)
XLA Modules:
  0.0 467.0 jit_solution(4847479925046069206)
XLA Ops:
  7.2 3.9 convert_add_fusion
  11.2 73.8 %reduce-scatter.3.cloned.1.call-done = f32[288,256]{1,0:T(8,128)} async-done(((f32[288,2048]{1,0:T(8,128)}), f32[288,256]{1,0:T(8,128)}) %reduce-scatter.3.cloned.1.call-update) | async-done | bytes 294928 | tf_op jit(solution)/shard_map/reduce_scatter | solution.py:48
  85.0 1.7 broadcast_multiply_fusion.1
  86.8 3.0 bitcast_convert_fusion
  89.8 50.6 %all-gather.3.cloned.1.call-done = f32[288,2048]{1,0:T(8,128)} async-done(((f32[288,256]{1,0:T(8,128)}), f32[288,2048]{1,0:T(8,128)}) %all-gather.3.cloned.1.call-update) | async-done | bytes 2359312 | tf_op jit(solution)/shard_map/all_gather | solution.py:52
  140.4 4.4 fusion.31
  144.9 68.0 %reduce-scatter.5.cloned.1.call-done = f32[288,256]{1,0:T(8,128)} async-done(((f32[288,2048]{1,0:T(8,128)}), f32[288,256]{1,0:T(8,128)}) %reduce-scatter.5.cloned.1.call-update) | async-done | bytes 294928 | tf_op jit(solution)/shard_map/reduce_scatter | solution.py:49
  212.9 1.7 broadcast_multiply_fusion
  214.6 0.6 all-reduce.6.cloned.1.call-start
  215.2 32.1 %all-reduce.4.cloned.1.call-done = f32[288,256]{1,0:T(8,128)} async-done(((f32[288,256]{1,0:T(8,128)}), f32[288,256]{1,0:T(8,128)}) %all-reduce.4.cloned.1.call-update) | async-done | bytes 294928 | tf_op jit(solution)/shard_map/psum | solution.py:59
  247.3 1.9 fusion.32
  249.4 11.7 %cholesky.130 = f32[128,128]{1,0:T(8,128)S(1)} custom-call(f32[128,128]{1,0:T(8,128)S(1)} %cholesky.194), custom_call_target="Cholesky" | custom-call | tf_op jit(solution)/shard_map/jit(cholesky)/cholesky | solution.py:19
  261.2 9.8 %custom-call.13 = f32[1,128,128]{1,2,0:T(8,128)S(1)} custom-call(f32[1,128,128]{2,1,0:T(8,128)S(1)} %get-tuple-element.48), custom_call_target="InvertDiagBlocksLowerTriangular" | custom-call | tf_op jit(solution)/shard_map/jit(cholesky)/cholesky | solution.py:19
  271.5 11.7 %cholesky.147 = f32[128,128]{1,0:T(8,128)S(1)} custom-call(f32[128,128]{1,0:T(8,128)S(1)} %convolution_subtract_fusion.3), custom_call_target="Cholesky" | custom-call | tf_op jit(solution)/shard_map/jit(cholesky)/cholesky | solution.py:19
  283.2 0.6 compare_reduce_fusion.2
  285.2 4.0 while.4
  285.4 0.6 fusion.54
  286.0 1.3 bitcast_dynamic-update-slice_fusion.4
  287.3 0.6 fusion.54
  287.9 1.3 bitcast_dynamic-update-slice_fusion.4
  289.2 19.7 %custom-call.14 = f32[2,128,128]{1,2,0:T(8,128)S(1)} custom-call(f32[2,128,128]{2,1,0:T(8,128)S(1)} %get-tuple-element.19), custom_call_target="InvertDiagBlocksLowerTriangular" | custom-call | tf_op jit(solution)/shard_map/jit(_solve_triangular)/triangular_solve | solution.py:20
  309.2 0.3 convolution_subtract_fusion.1
  309.8 8.1 %multiply_reduce_fusion.1 = (f32[256]{0:T(256)S(1)}, f32[2048,256]{1,0:T(8,128)}) fusion(f32[288,2048]{1,0:T(8,128)} %all-gather.3.cloned.1.call-done, f32[128,288]{0,1:T(8,128)S(1)} %fusion.18, f32[128,288]{0,1:T(8,128)S(1)} %fusion.11), kind=kOutput, calls=%fused_computation.15 | convolution fusion | flops 1813061376 | bytes 4752384 | tf_op jit(solution)/shard_map/dot_general | solution.py:24
  317.9 5.9 %psum.29 = f32[256]{0:T(256)S(1)} all-reduce(f32[256]{0:T(256)S(1)} %get-tuple-element.51), channel_id=1, replica_groups=mesh['rep'=8,'col'=4] {'col'}, use_global_device_ids=true, to_apply=%region_7.0 | all-reduce | flops 256 | bytes 2048 | tf_op jit(solution)/shard_map/psum | solution.py:29
  323.8 5.2 %convolution_multiply_fusion.2 = f32[288,2048]{1,0:T(8,128)} fusion(f32[2048,256]{1,0:T(8,128)} %get-tuple-element.52, f32[128,288]{0,1:T(8,128)S(1)} %fusion.18, f32[128,288]{0,1:T(8,128)S(1)} %fusion.11), kind=kOutput, calls=%fused_computation.9 | convolution fusion | flops 1812602880 | bytes 4751360 | tf_op jit(solution)/shard_map/dot_general | solution.py:34
  329.0 6.7 %fusion.4 = f32[288,256]{1,0:T(8,128)} fusion(f32[2048,256]{1,0:T(8,128)} %get-tuple-element.52, f32[256]{0:T(256)S(1)} %add_sqrt_fusion.1, f32[288,2048]{1,0:T(8,128)} %all-gather.5.cloned.1.call-done, f32[288,2048]{1,0:T(8,128)} %all-gather.3.cloned.1.call-done, f32[288,2048]{1,0:T(8,128)} %convolution_multiply_fusion.2), kind=kOutput, calls=%fused_computation.23 | convolution fusion | flops 1813643264 | bytes 9470976 | tf_op jit(solution)/shard_map/dot_general | solution.py:59
  335.7 5.9 %fusion.3 = f32[288,2048]{1,0:T(8,128)} fusion(f32[288,2048]{1,0:T(8,128)} %param.9, f32[2048,256]{1,0:T(8,128)} %get-tuple-element.52, f32[256]{0:T(256)S(1)} %add_sqrt_fusion.1, f32[128,288]{0,1:T(8,128)S(1)} %fusion.18, f32[128,288]{0,1:T(8,128)S(1)} %fusion.11), kind=kOutput, calls=%fused_computation.11 | convolution fusion | flops 1813716992 | bytes 7111680 | tf_op jit(solution)/shard_map/dot_general | solution.py:38
  341.6 26.8 %all-reduce.6.cloned.1.call-done = f32[288,256]{1,0:T(8,128)} async-done(((f32[288,256]{1,0:T(8,128)}), f32[288,256]{1,0:T(8,128)}) %all-reduce.6.cloned.1.call-update) | async-done | bytes 294928 | tf_op jit(solution)/shard_map/psum | solution.py:59
  368.4 1.9 fusion.33
  370.6 11.7 %cholesky.164 = f32[128,128]{1,0:T(8,128)S(1)} custom-call(f32[128,128]{1,0:T(8,128)S(1)} %cholesky.197), custom_call_target="Cholesky" | custom-call | tf_op jit(solution)/shard_map/jit(cholesky)/cholesky | solution.py:19
  382.3 10.2 %custom-call.15 = f32[1,128,128]{1,2,0:T(8,128)S(1)} custom-call(f32[1,128,128]{2,1,0:T(8,128)S(1)} %get-tuple-element.44), custom_call_target="InvertDiagBlocksLowerTriangular" | custom-call | tf_op jit(solution)/shard_map/jit(cholesky)/cholesky | solution.py:19
  393.0 11.7 %cholesky.181 = f32[128,128]{1,0:T(8,128)S(1)} custom-call(f32[128,128]{1,0:T(8,128)S(1)} %convolution_subtract_fusion.2), custom_call_target="Cholesky" | custom-call | tf_op jit(solution)/shard_map/jit(cholesky)/cholesky | solution.py:19
  404.7 0.6 compare_reduce_fusion.1
  405.4 0.7 compare_reduce_fusion
  407.4 3.9 while.5
  407.4 0.6 fusion.55
  408.0 1.3 bitcast_dynamic-update-slice_fusion.5
  409.4 0.6 fusion.55
  410.0 1.3 bitcast_dynamic-update-slice_fusion.5
  411.3 19.8 %custom-call.16 = f32[2,128,128]{1,2,0:T(8,128)S(1)} custom-call(f32[2,128,128]{2,1,0:T(8,128)S(1)} %get-tuple-element.20), custom_call_target="InvertDiagBlocksLowerTriangular" | custom-call | tf_op jit(solution)/shard_map/jit(_solve_triangular)/triangular_solve | solution.py:20
  431.2 0.3 fusion.9
  431.5 0.3 convolution_subtract_fusion
  431.8 0.3 fusion.14
  432.0 9.5 %multiply_reduce_fusion = (f32[256]{0:T(256)S(1)}, f32[2048,256]{1,0:T(8,128)}) fusion(f32[128,288]{0,1:T(8,128)S(1)} %fusion.14, f32[128,288]{0,1:T(8,128)S(1)} %fusion.9, f32[288,2048]{1,0:T(8,128)} %all-gather.5.cloned.1.call-done, f32[288,2048]{1,0:T(8,128)} %all-gather.3.cloned.1.call-done, f32[288,2048]{1,0:T(8,128)} %convolution_multiply_fusion.2), kind=kOutput, calls=%fused_computation.14 | convolution fusion | flops 1814241024 | bytes 9470976 | tf_op jit(solution)/shard_map/dot_general | solution.py:24
  441.6 5.7 %psum.31 = f32[256]{0:T(256)S(1)} all-reduce(f32[256]{0:T(256)S(1)} %get-tuple-element.55), channel_id=1, replica_groups=mesh['rep'=8,'col'=4] {'col'}, use_global_device_ids=true, to_apply=%region_11.14 | all-reduce | flops 256 | bytes 2048 | tf_op jit(solution)/shard_map/psum | solution.py:29
  447.3 7.2 %fusion.1 = f32[1,288,2048]{2,1,0:T(8,128)} fusion(f32[2048,256]{1,0:T(8,128)} %get-tuple-element.56, f32[288,2048]{1,0:T(8,128)} %convert_add_fusion, f32[288,2048]{1,0:T(8,128)} %convolution_multiply_fusion.2, bf16[2,1,288,2048]{3,2,1,0:T(8,128)(2,1)} %param.8, f32[128,288]{0,1:T(8,128)S(1)} %fusion.14, f32[128,288]{0,1:T(8,128)S(1)} %fusion.9), kind=kOutput, calls=%fused_computation.6 | convolution fusion | flops 1814962176 | bytes 10649600 | tf_op jit(solution)/shard_map/dot_general | solution.py:34
  454.7 1.5 copy-done.5
  456.2 3.8 fusion.2
  (54 shorter events, 2.7 us)
Async XLA Ops:
  7.2 133.2 %copy-start = (f32[2048,256]{1,0:T(8,128)S(1)}, f32[2048,256]{1,0:T(8,128)}, u32[]{:S(2)}) copy-start(f32[2048,256]{1,0:T(8,128)} %param.10) | copy-start | bytes 6291460
  7.2 77.8 %reduce-scatter.3.cloned.1.call-start = ((), (), s32[]{:S(2)}) async-start(), calls=%async_computation.2 | async-start | bytes 2654208 | tf_op jit(solution)/shard_map/reduce_scatter | solution.py:48
  11.2 129.2 %all-gather.3.cloned.1.call-start = ((), (), s32[]{:S(2)}) async-start(), calls=%async_computation.3 | async-start | bytes 2654208 | tf_op jit(solution)/shard_map/all_gather | solution.py:52
  86.7 126.2 %reduce-scatter.5.cloned.1.call-start = ((), (), s32[]{:S(2)}) async-start(), calls=%async_computation.5 | async-start | bytes 2654208 | tf_op jit(solution)/shard_map/reduce_scatter | solution.py:49
  89.8 157.5 %all-reduce.4.cloned.1.call-start = ((), (), s32[]{:S(2)}) async-start(), calls=%async_computation.4 | async-start | bytes 589824 | tf_op jit(solution)/shard_map/psum | solution.py:59
  144.9 184.1 %all-gather.5.cloned.1.call-start = ((), (), s32[]{:S(2)}) async-start(), calls=%async_computation.6 | async-start | bytes 2654208 | tf_op jit(solution)/shard_map/all_gather | solution.py:53
  214.6 153.8 %all-reduce.6.cloned.1.call-start = ((), (), s32[]{:S(2)}) async-start(), calls=%async_computation.7 | async-start | bytes 589824 | tf_op jit(solution)/shard_map/psum | solution.py:59
  247.3 61.6 %copy-start.3 = (f32[288,256]{1,0:T(8,128)S(1)}, f32[288,256]{1,0:T(8,128)}, u32[]{:S(2)}) copy-start(f32[288,256]{1,0:T(8,128)} %all-reduce.4.cloned.1.call-done) | copy-start | bytes 884740
  368.4 62.7 %copy-start.4 = (f32[288,256]{1,0:T(8,128)S(1)}, f32[288,256]{1,0:T(8,128)}, u32[]{:S(2)}) copy-start(f32[288,256]{1,0:T(8,128)} %all-reduce.6.cloned.1.call-done) | copy-start | bytes 884740
  447.3 7.2 %copy-start.1 = (f32[2048,256]{1,0:T(8,128)S(1)}, f32[2048,256]{1,0:T(8,128)}, u32[]{:S(2)}) copy-start(f32[2048,256]{1,0:T(8,128)} %get-tuple-element.56) | copy-start | bytes 6291460
  454.6 1.7 copy-start.5
  456.2 3.8 copy-start.2
Sparse Core Ops, SparseCore 0:
  12.1 72.8 reduce-scatter.2
  87.6 52.7 all-gather.2
  144.5 68.3 reduce-scatter.4
  215.7 31.5 all-reduce.3
  249.8 53.9 all-gather.4
  335.8 32.5 all-reduce.5
where the time goes:
time: 470 us; the launch traced here: 467 us
  waiting for transfers between devices  251 us (53%)
  other arithmetic  119 us (25%)
  matrix products  57.3 us (12%)
  between operations  17.1 us (4%)
  blocking collectives  11.6 us (2%)
  local copies, waits for them, and re-layouts  9.61 us (2%)
    reduce_scatter x1, waiting for transfers between devices, shards(): lax.psum_scatter(first_sum, 'rep', scatter_dimension=1, tiled=True)  73.8 us
    another operation x13, other arithmetic, orthonormal(): lower_factor = jnp.linalg.cholesky(gram_matrix)  68.9 us
    reduce_scatter x1, waiting for transfers between devices, shards(): lax.psum_scatter(grads[1, 0].astype(jnp.float32), 'rep', scatter_dimensio...  68 us
    psum x2, waiting for transfers between devices, shards(): lax.psum(jnp.dot(averaged, right_factor, precision=precise), 'col')  58.9 us
    all_gather x1, waiting for transfers between devices, shards(): lax.all_gather(summed[0] / replicas, 'rep', axis=1, tiled=True)  50.6 us
    another operation x5, other arithmetic, orthonormal(): jax.scipy.linalg.solve_triangular(lower_factor, left_raw.T, lower=True)  39.6 us
    dot_general x2, matrix products, transposed(): lax.dot_general(matrix, left_factor, (((0,), (0,)), ((), ())), precision=...  17.6 us
    dot_general x2, matrix products, finish(): correction = jnp.dot(left_factor, right_raw.T, precision=precise)  12.4 us
  transfers between devices with their start and end apart: 6, of which 5 were waited for; matrix products, arithmetic and copies ran while one was open for 19% of the time, Pallas kernels for 0%

commit v1 on v0

--- a/solution.py
+++ b/solution.py
@@ -56,7 +56,9 @@
     for section_index in range(STEPS):
         if section_index > 0:
             combined = moment + grads[section_index, 0].astype(jnp.float32)
-        left_raw = lax.psum(jnp.dot(averaged, right_factor, precision=precise), "col")
+        left_raw = jnp.sum(
+            lax.all_gather(jnp.dot(averaged, right_factor, precision=precise), "col"), axis=0
+        )
         left_factor = orthonormal(left_raw)
         right_raw = transposed(averaged, left_factor)
         moment, right_factor, weight_now, correction = finish(

time: 470 us -> 441 us (0.938)
  waiting for transfers between devices: 251 us -> 222 us
    psum x2 -> x0, waiting for transfers between devices: 58.9 us -> none  [shards(): lax.psum(jnp.dot(averaged, right_factor, precision=precise), 'col')]
    all_gather x0 -> x2, waiting for transfers between devices: none -> 29.1 us  [shards(): lax.all_gather(jnp.dot(averaged, right_factor, precision=precise), 'col')]
  transfers between devices with their start and end apart: 6 -> 6, of which waited for: 5 -> 5; matrix products, arithmetic and copies ran while one was open for 19% -> 20% of each run, Pallas kernels for 0% -> 0%
where the time goes in v1:
time: 441 us; the launch traced here: 438 us
  waiting for transfers between devices  222 us (50%)
  other arithmetic  122 us (28%)
  matrix products  55.1 us (12%)
  between operations  17.1 us (4%)
  blocking collectives  11.9 us (3%)
  local copies, waits for them, and re-layouts  9.61 us (2%)
    reduce_scatter x1, waiting for transfers between devices, shards(): lax.psum_scatter(first_sum, 'rep', scatter_dimension=1, tiled=True)  73.8 us
    another operation x13, other arithmetic, orthonormal(): lower_factor = jnp.linalg.cholesky(gram_matrix)  68.9 us
    reduce_scatter x1, waiting for transfers between devices, shards(): lax.psum_scatter(grads[1, 0].astype(jnp.float32), 'rep', scatter_dimensio...  68 us
    all_gather x1, waiting for transfers between devices, shards(): lax.all_gather(summed[0] / replicas, 'rep', axis=1, tiled=True)  50.6 us
    another operation x5, other arithmetic, orthonormal(): jax.scipy.linalg.solve_triangular(lower_factor, left_raw.T, lower=True)  39.6 us
    all_gather x2, waiting for transfers between devices, shards(): lax.all_gather(jnp.dot(averaged, right_factor, precision=precise), 'col')  29.1 us
    dot_general x2, matrix products, transposed(): lax.dot_general(matrix, left_factor, (((0,), (0,)), ((), ())), precision=...  17.6 us
    dot_general x2, matrix products, finish(): correction = jnp.dot(left_factor, right_raw.T, precision=precise)  12.4 us
  transfers between devices with their start and end apart: 6, of which 5 were waited for; matrix products, arithmetic and copies ran while one was open for 20% of the time, Pallas kernels for 0%

profile of v1, /device:TPU:0, one launch (start us, length us, event | category | flops | bytes accessed | tf_op | source)
XLA Modules:
  0.0 438.0 jit_solution(10321939123865134825)
XLA Ops:
  7.2 3.9 convert_add_fusion
  11.2 73.8 %reduce-scatter.3.cloned.1.call-done = f32[288,256]{1,0:T(8,128)} async-done(((f32[288,2048]{1,0:T(8,128)}), f32[288,256]{1,0:T(8,128)}) %reduce-scatter.3.cloned.1.call-update) | async-done | bytes 294928 | tf_op jit(solution)/shard_map/reduce_scatter | solution.py:48
  85.0 1.7 broadcast_multiply_fusion.1
  86.8 3.0 bitcast_convert_fusion
  89.8 50.6 %all-gather.7.cloned.1.call-done = f32[288,2048]{1,0:T(8,128)} async-done(((f32[288,256]{1,0:T(8,128)}), f32[288,2048]{1,0:T(8,128)}) %all-gather.7.cloned.1.call-update) | async-done | bytes 2359312 | tf_op jit(solution)/shard_map/all_gather | solution.py:52
  140.4 4.4 %fusion.31 = f32[288,256]{1,0:T(8,128)} fusion(f32[288,2048]{1,0:T(8,128)} %all-gather.7.cloned.1.call-done, f32[2048,256]{1,0:T(8,128)S(1)} %copy-done), kind=kOutput, calls=%fused_computation.82 | convolution fusion | flops 1811939328 | bytes 4751360 | tf_op jit(solution)/shard_map/dot_general | solution.py:60
  144.9 68.0 %reduce-scatter.5.cloned.1.call-done = f32[288,256]{1,0:T(8,128)} async-done(((f32[288,2048]{1,0:T(8,128)}), f32[288,256]{1,0:T(8,128)}) %reduce-scatter.5.cloned.1.call-update) | async-done | bytes 294928 | tf_op jit(solution)/shard_map/reduce_scatter | solution.py:49
  212.9 1.7 broadcast_multiply_fusion
  214.6 0.6 all-gather.13.cloned.1.call-start
  215.2 16.3 %all-gather.11.cloned.1.call-done = f32[1152,256]{1,0:T(8,128)} async-done(((f32[288,256]{1,0:T(8,128)}), f32[1152,256]{1,0:T(8,128)}) %all-gather.11.cloned.1.call-update) | async-done | bytes 1179664 | tf_op jit(solution)/shard_map/all_gather | solution.py:60
  231.5 1.4 reduce_sum.36
  232.9 0.8 fusion.32
  233.9 11.7 %cholesky.130 = f32[128,128]{1,0:T(8,128)S(1)} custom-call(f32[128,128]{1,0:T(8,128)S(1)} %cholesky.194), custom_call_target="Cholesky" | custom-call | tf_op jit(solution)/shard_map/jit(cholesky)/cholesky | solution.py:19
  245.7 9.8 %custom-call.13 = f32[1,128,128]{1,2,0:T(8,128)S(1)} custom-call(f32[1,128,128]{2,1,0:T(8,128)S(1)} %get-tuple-element.48), custom_call_target="InvertDiagBlocksLowerTriangular" | custom-call | tf_op jit(solution)/shard_map/jit(cholesky)/cholesky | solution.py:19
  256.0 11.7 %cholesky.147 = f32[128,128]{1,0:T(8,128)S(1)} custom-call(f32[128,128]{1,0:T(8,128)S(1)} %convolution_subtract_fusion.3), custom_call_target="Cholesky" | custom-call | tf_op jit(solution)/shard_map/jit(cholesky)/cholesky | solution.py:19
  267.8 0.6 compare_reduce_fusion.2
  269.7 4.0 while.4
  269.9 0.6 fusion.54
  270.5 1.3 bitcast_dynamic-update-slice_fusion.4
  271.8 0.6 fusion.54
  272.4 1.3 bitcast_dynamic-update-slice_fusion.4
  273.7 19.7 %custom-call.14 = f32[2,128,128]{1,2,0:T(8,128)S(1)} custom-call(f32[2,128,128]{2,1,0:T(8,128)S(1)} %get-tuple-element.19), custom_call_target="InvertDiagBlocksLowerTriangular" | custom-call | tf_op jit(solution)/shard_map/jit(_solve_triangular)/triangular_solve | solution.py:20
  293.7 0.3 convolution_subtract_fusion.1
  294.2 8.1 %multiply_reduce_fusion.1 = (f32[256]{0:T(256)S(1)}, f32[2048,256]{1,0:T(8,128)}) fusion(f32[288,2048]{1,0:T(8,128)} %all-gather.7.cloned.1.call-done, f32[128,288]{0,1:T(8,128)S(1)} %fusion.18, f32[128,288]{0,1:T(8,128)S(1)} %fusion.11), kind=kOutput, calls=%fused_computation.15 | convolution fusion | flops 1813061376 | bytes 4752384 | tf_op jit(solution)/shard_map/dot_general | solution.py:24
  302.3 6.0 %psum.14 = f32[256]{0:T(256)S(1)} all-reduce(f32[256]{0:T(256)S(1)} %get-tuple-element.51), channel_id=1, replica_groups=mesh['rep'=8,'col'=4] {'col'}, use_global_device_ids=true, to_apply=%region_7.0 | all-reduce | flops 256 | bytes 2048 | tf_op jit(solution)/shard_map/psum | solution.py:29
  308.4 5.2 %convolution_multiply_fusion.2 = f32[288,2048]{1,0:T(8,128)} fusion(f32[2048,256]{1,0:T(8,128)} %get-tuple-element.52, f32[128,288]{0,1:T(8,128)S(1)} %fusion.18, f32[128,288]{0,1:T(8,128)S(1)} %fusion.11), kind=kOutput, calls=%fused_computation.9 | convolution fusion | flops 1812602880 | bytes 4751360 | tf_op jit(solution)/shard_map/dot_general | solution.py:34
  313.6 6.7 %fusion.4 = f32[288,256]{1,0:T(8,128)} fusion(f32[2048,256]{1,0:T(8,128)} %get-tuple-element.52, f32[256]{0:T(256)S(1)} %add_sqrt_fusion.1, f32[288,2048]{1,0:T(8,128)} %all-gather.9.cloned.1.call-done, f32[288,2048]{1,0:T(8,128)} %all-gather.7.cloned.1.call-done, f32[288,2048]{1,0:T(8,128)} %convolution_multiply_fusion.2), kind=kOutput, calls=%fused_computation.23 | convolution fusion | flops 1813643264 | bytes 9470976 | tf_op jit(solution)/shard_map/dot_general | solution.py:60
  320.3 5.9 %fusion.3 = f32[288,2048]{1,0:T(8,128)} fusion(f32[288,2048]{1,0:T(8,128)} %param.9, f32[2048,256]{1,0:T(8,128)} %get-tuple-element.52, f32[256]{0:T(256)S(1)} %add_sqrt_fusion.1, f32[128,288]{0,1:T(8,128)S(1)} %fusion.18, f32[128,288]{0,1:T(8,128)S(1)} %fusion.11), kind=kOutput, calls=%fused_computation.11 | convolution fusion | flops 1813716992 | bytes 7111680 | tf_op jit(solution)/shard_map/dot_general | solution.py:38
  326.2 12.8 %all-gather.13.cloned.1.call-done = f32[1152,256]{1,0:T(8,128)} async-done(((f32[288,256]{1,0:T(8,128)}), f32[1152,256]{1,0:T(8,128)}) %all-gather.13.cloned.1.call-update) | async-done | bytes 1179664 | tf_op jit(solution)/shard_map/all_gather | solution.py:60
  339.0 1.4 reduce_sum.38
  340.4 0.8 fusion.33
  341.4 11.7 %cholesky.164 = f32[128,128]{1,0:T(8,128)S(1)} custom-call(f32[128,128]{1,0:T(8,128)S(1)} %cholesky.197), custom_call_target="Cholesky" | custom-call | tf_op jit(solution)/shard_map/jit(cholesky)/cholesky | solution.py:19
  353.2 10.2 %custom-call.15 = f32[1,128,128]{1,2,0:T(8,128)S(1)} custom-call(f32[1,128,128]{2,1,0:T(8,128)S(1)} %get-tuple-element.44), custom_call_target="InvertDiagBlocksLowerTriangular" | custom-call | tf_op jit(solution)/shard_map/jit(cholesky)/cholesky | solution.py:19
  363.8 11.7 %cholesky.181 = f32[128,128]{1,0:T(8,128)S(1)} custom-call(f32[128,128]{1,0:T(8,128)S(1)} %convolution_subtract_fusion.2), custom_call_target="Cholesky" | custom-call | tf_op jit(solution)/shard_map/jit(cholesky)/cholesky | solution.py:19
  375.5 0.6 compare_reduce_fusion.1
  376.2 0.7 compare_reduce_fusion
  378.2 4.0 while.5
  378.3 0.6 fusion.55
  378.8 1.4 bitcast_dynamic-update-slice_fusion.5
  380.2 0.6 fusion.55
  380.8 1.4 bitcast_dynamic-update-slice_fusion.5
  382.2 19.8 %custom-call.16 = f32[2,128,128]{1,2,0:T(8,128)S(1)} custom-call(f32[2,128,128]{2,1,0:T(8,128)S(1)} %get-tuple-element.20), custom_call_target="InvertDiagBlocksLowerTriangular" | custom-call | tf_op jit(solution)/shard_map/jit(_solve_triangular)/triangular_solve | solution.py:20
  402.3 0.3 convolution_subtract_fusion
  402.9 9.5 %multiply_reduce_fusion = (f32[256]{0:T(256)S(1)}, f32[2048,256]{1,0:T(8,128)}) fusion(f32[128,288]{0,1:T(8,128)S(1)} %fusion.14, f32[128,288]{0,1:T(8,128)S(1)} %fusion.9, f32[288,2048]{1,0:T(8,128)} %all-gather.9.cloned.1.call-done, f32[288,2048]{1,0:T(8,128)} %all-gather.7.cloned.1.call-done, f32[288,2048]{1,0:T(8,128)} %convolution_multiply_fusion.2), kind=kOutput, calls=%fused_computation.14 | convolution fusion | flops 1814241024 | bytes 9470976 | tf_op jit(solution)/shard_map/dot_general | solution.py:24
  412.5 5.8 %psum.15 = f32[256]{0:T(256)S(1)} all-reduce(f32[256]{0:T(256)S(1)} %get-tuple-element.55), channel_id=1, replica_groups=mesh['rep'=8,'col'=4] {'col'}, use_global_device_ids=true, to_apply=%region_11.14 | all-reduce | flops 256 | bytes 2048 | tf_op jit(solution)/shard_map/psum | solution.py:29
  418.3 7.2 %fusion.1 = f32[1,288,2048]{2,1,0:T(8,128)} fusion(f32[2048,256]{1,0:T(8,128)} %get-tuple-element.56, f32[288,2048]{1,0:T(8,128)} %convert_add_fusion, f32[288,2048]{1,0:T(8,128)} %convolution_multiply_fusion.2, bf16[2,1,288,2048]{3,2,1,0:T(8,128)(2,1)} %param.8, f32[128,288]{0,1:T(8,128)S(1)} %fusion.14, f32[128,288]{0,1:T(8,128)S(1)} %fusion.9), kind=kOutput, calls=%fused_computation.6 | convolution fusion | flops 1814962176 | bytes 10649600 | tf_op jit(solution)/shard_map/dot_general | solution.py:34
  425.7 1.5 copy-done.3
  427.2 3.8 fusion.2
  (52 shorter events, 3.2 us)
Async XLA Ops:
  7.2 133.2 %copy-start = (f32[2048,256]{1,0:T(8,128)S(1)}, f32[2048,256]{1,0:T(8,128)}, u32[]{:S(2)}) copy-start(f32[2048,256]{1,0:T(8,128)} %param.10) | copy-start | bytes 6291460
  7.2 77.8 %reduce-scatter.3.cloned.1.call-start = ((), (), s32[]{:S(2)}) async-start(), calls=%async_computation.2 | async-start | bytes 2654208 | tf_op jit(solution)/shard_map/reduce_scatter | solution.py:48
  11.2 129.2 %all-gather.7.cloned.1.call-start = ((), (), s32[]{:S(2)}) async-start(), calls=%async_computation.3 | async-start | bytes 2654208 | tf_op jit(solution)/shard_map/all_gather | solution.py:52
  86.7 126.2 %reduce-scatter.5.cloned.1.call-start = ((), (), s32[]{:S(2)}) async-start(), calls=%async_computation.4 | async-start | bytes 2654208 | tf_op jit(solution)/shard_map/reduce_scatter | solution.py:49
  89.8 141.8 %all-gather.11.cloned.1.call-start = ((), (), s32[]{:S(2)}) async-start(), calls=%async_computation.6 | async-start | bytes 1474560 | tf_op jit(solution)/shard_map/all_gather | solution.py:60
  144.9 168.7 %all-gather.9.cloned.1.call-start = ((), (), s32[]{:S(2)}) async-start(), calls=%async_computation.5 | async-start | bytes 2654208 | tf_op jit(solution)/shard_map/all_gather | solution.py:53
  214.6 124.4 %all-gather.13.cloned.1.call-start = ((), (), s32[]{:S(2)}) async-start(), calls=%async_computation.7 | async-start | bytes 1474560 | tf_op jit(solution)/shard_map/all_gather | solution.py:60
  418.3 7.2 %copy-start.1 = (f32[2048,256]{1,0:T(8,128)S(1)}, f32[2048,256]{1,0:T(8,128)}, u32[]{:S(2)}) copy-start(f32[2048,256]{1,0:T(8,128)} %get-tuple-element.56) | copy-start | bytes 6291460
  425.6 1.7 copy-start.3
  427.2 3.8 copy-start.2
Sparse Core Ops, SparseCore 0:
  12.1 72.8 reduce-scatter.2
  87.6 52.7 all-gather.6
  144.5 68.3 reduce-scatter.4
  214.9 16.5 all-gather.10
  234.0 53.3 all-gather.8
  320.5 18.4 all-gather.12
